TPU v7x, 32 devices: a whole 2x2x4 slice. The times are simulated.
32 devices in a mesh: grp: 2 (over x), slc: 16 (over z, y, core).
Axes of the slice: x: 2, y: 2, z: 4, core: 2. Of those that a mesh axis runs over, the one named last changes fastest.
Arguments:
- bitstrings: int32 [1024], P('grp'), parts along dimension 0, may hold values from 0 to 511, as said below
- tree_order: int32 [12], P('grp'), parts along dimension 0, may hold values from 0 to 5, each once
- owners: int32 [12], P('grp'), parts along dimension 0, may hold values from 0 to 15
- slice_assign: int32 [64, 6], P(('grp', 'slc')), parts along dimension 0, may hold values from 0 to 63
- boundary: bfloat16 [1024, 4096], P('grp'), parts along dimension 0, may hold values from -6 to 6
- branch_pool: bfloat16 [32, 64, 4096], P(('grp', 'slc')), parts along dimension 0, may hold values from -0.75 to 0.75
- slice_tensors: bfloat16 [12, 64, 4096], P('grp'), parts along dimension 0, may hold values from -3 to 3
- closing: bfloat16 [8192, 128], P('grp'), parts along dimension 0, may hold values from -0.09375 to 0.09375
Outputs:
- amplitudes: float32 [1024, 128], P(('grp', 'slc')), parts along dimension 0
There are 2 independent parts, one for each index of `grp`. A program takes and returns all parts, laid end to end along the dimension named above; each array names one. Nothing has to cross between parts.
Inputs may be any that keep to these rules, and one draw needn't show every extreme that they name: `bitstrings`: 512 distinct configurations. `tree_order`: a permutation of the sections.
All inputs are finite; a program needn't handle non-finite values.
Results may differ from a plain program's by a relative error of at most 0.0075.
Values may be sent and summed in bfloat16 or wider, within the bound.
A program may use at most 128 MiB of HBM per device.

v0:
```python
import math
import jax
import jax.numpy as jnp
from jax import lax
from jax.sharding import PartitionSpec as P


def spread(block, axis, owner):
    block = jnp.where(lax.axis_index(axis) == owner, block, jnp.zeros_like(block))
    return lax.psum(block, axis)


def local(
    bitstrings, tree_order, owners, slice_assign, boundary, branch_pool, slice_tensors, closing
):
    group_count = lax.axis_size("slc")
    my_index = lax.axis_index("slc")
    slice_count = slice_assign.shape[0]
    bond_dim = branch_pool.shape[1]
    pair_dim = branch_pool.shape[2]
    row_total = bitstrings.shape[0]
    section_count = tree_order.shape[0]
    starts = jnp.take(boundary, bitstrings, axis=0)
    states = jnp.broadcast_to(starts[None], (slice_count, row_total, pair_dim))
    own_branch = branch_pool[0]
    for section_idx in range(section_count):
        branch = spread(own_branch, "slc", owners[section_idx])
        product = jnp.einsum(
            "srab,acb->srcb",
            states.reshape(slice_count, row_total, bond_dim, bond_dim),
            branch.reshape(bond_dim, bond_dim, bond_dim),
            preferred_element_type=jnp.float32,
        )
        table = lax.dynamic_index_in_dim(slice_tensors, tree_order[section_idx], 0, keepdims=False)
        factor = jnp.take(table, slice_assign[:, section_idx], axis=0).astype(jnp.float32)
        states = (product.reshape(slice_count, row_total, pair_dim) * factor[:, None, :]).astype(
            jnp.bfloat16
        )
    inverse = 1.0 / math.sqrt(slice_count * group_count)
    share_rows = row_total // group_count
    partial_amps = jnp.einsum("srw,wo->ro", states, closing, preferred_element_type=jnp.float32)
    totals = lax.psum(partial_amps, "slc")
    summed = lax.dynamic_slice_in_dim(totals, my_index * share_rows, share_rows, 0)
    return summed * inverse


def solution(mesh):
    return jax.shard_map(
        local,
        mesh=mesh,
        in_specs=(
            P("grp"),
            P("grp"),
            P("grp"),
            P(("grp", "slc"), None),
            P("grp", None),
            P(("grp", "slc"), None, None),
            P("grp", None, None),
            P("grp", None),
        ),
        out_specs=P(("grp", "slc"), None),
        check_vma=False,
    )
```

profile of v0, /device:TPU:0, one launch (start us, length us, event | category | flops | bytes accessed | tf_op | source)
XLA Modules:
  0.0 318.7 jit_solution(11319033203107848922)
XLA Ops:
  6.5 0.0 copy-start
  6.5 0.0 all-reduce.6.cloned.1.call-start
  6.5 1.5 fusion.25
  11.9 2.4 broadcast_select_fusion.6
  14.3 2.1 reshape.99
  16.3 2.9 copy.34
  19.3 2.1 reshape.102
  21.3 2.9 copy.37
  24.2 2.1 reshape.101
  26.3 2.9 copy.36
  29.2 2.1 reshape.100
  31.3 2.9 copy.35
  34.2 1.1 reshape.104
  35.3 2.9 copy.39
  38.2 1.1 reshape.103
  39.4 0.0 copy-start.5
  39.4 2.9 copy.38
  42.3 0.0 all-reduce.6.cloned.1.call-update
  42.3 0.2 all-reduce.4.cloned.1.call-start
  42.6 0.0 copy-done.4
  42.6 0.7 fusion.24
  50.8 0.0 copy-done.3
  50.8 0.3 slice_reduce_fusion.1
  55.0 3.2 dynamic-slice_bitcast_fusion.1
  58.2 1.7 gather_fusion.5
  59.9 0.1 fusion.22
  60.0 0.1 reshape.115
  60.1 0.1 copy.46
  60.2 1.7 gather_fusion.4
  61.9 0.1 fusion.21
  62.0 0.1 reshape.114
  62.1 0.1 copy.45
  62.2 0.6 gather_fusion.3
  62.8 0.1 fusion.20
  62.9 0.1 reshape.113
  63.0 0.1 copy.44
  63.1 0.6 gather_fusion.2
  63.6 0.1 fusion.19
  63.7 0.1 reshape.112
  63.8 0.1 copy.43
  63.9 0.6 gather_fusion.1
  64.5 0.1 fusion.18
  64.6 0.1 reshape.111
  64.7 0.1 copy.42
  64.8 0.6 gather_fusion.6
  65.4 0.1 fusion.23
  65.5 0.1 reshape.116
  65.6 0.1 copy.47
  65.7 0.0 copy-done.5
  65.7 11.4 %gather_fusion = bf16[512,4096]{1,0:T(8,128)(2,1)} fusion(bf16[512,4096]{1,0:T(8,128)(2,1)} %param.14, s32[1024]{0:T(1024)S(1)} %pad_clamp_fusion.6), kind=kCustom, calls=%fused_computation.6 | custom fusion | bytes 8390656 | tf_op jit(solution)/shard_map/jit(_take)/gather | solution.py:23
  77.1 6.5 %copy.40 = bf16[512,4096]{0,1:T(8,128)(2,1)} copy(bf16[512,4096]{1,0:T(8,128)(2,1)} %gather_fusion) | data formatting | bytes 8388608 | tf_op jit(solution)/shard_map/jit(_take)/gather | solution.py:23
  83.6 2.7 broadcast_select_fusion
  86.3 4.4 %copy.41 = bf16[512,64,64]{0,1,2:T(8,128)(2,1)} copy(bf16[512,64,64]{0,2,1:T(8,128)(2,1)S(1)} %broadcast_select_fusion) | data formatting | bytes 8388608 | tf_op jit(solution)/shard_map/jit(_take)/select_n | solution.py:23
  90.7 94.3 %all-reduce.6.cloned.1.call-done = (bf16[64,64,64]{0,1,2:T(8,128)(2,1)}, bf16[64,64,64]{0,1,2:T(8,128)(2,1)}, bf16[64,64,64]{0,1,2:T(8,128)(2,1)}, bf16[64,64,64...) async-done(((bf16[64,64,64]{0,1,2:T(8,128)(2,1)}, bf16[64,64,64]{0,1,2:T(8,128)(2,1)}, bf16[64,64,64]{0,1,2:T(8,128)(2,1)}, ...) | async-done | bytes 3145744 | tf_op jit(solution)/shard_map/psum | solution.py:10
  185.0 8.7 %fusion.4 = bf16[2,512,64,64]{1,2,0,3:T(8,128)(2,1)} fusion(f32[2,64,64]{1,0,2:T(2,128)S(1)} %copy.43, f32[2,64,64]{1,0,2:T(2,128)S(1)} %copy.42, bf16[512,64,64]{0,1,2:T(8,128)(2,1)} %copy.41, bf16[64,64,64]{0,1,2:T(8,128)(2,1)} %get-tuple-element.12, bf16[64,64,64]{0,1,2:T(8,128)(2,1)} %get-tuple-element.13), kind=kOutput, calls=%fused_computation.16 | convolution fusion | flops 1090519040 | bytes 13697024 | tf_op jit(solution)/shard_map/srab,acb->srcb/dot_general | solution.py:28
  193.7 0.0 copy-done.1
  193.7 0.0 copy-done.2
  193.7 9.8 %fusion.2 = bf16[2,512,64,64]{1,2,0,3:T(8,128)(2,1)} fusion(f32[2,64,64]{1,0,2:T(2,128)S(1)} %copy.45, bf16[2,512,64,64]{1,2,0,3:T(8,128)(2,1)} %fusion.4, f32[2,64,64]{1,0,2:T(2,128)S(1)} %copy.44, bf16[64,64,64]{0,1,2:T(8,128)(2,1)S(1)} %copy-done.1, bf16[64,64,64]{0,1,2:T(8,128)(2,1)S(1)} %copy-done.2), kind=kOutput, calls=%fused_computation.12 | convolution fusion | flops 1090519040 | bytes 17891328 | tf_op jit(solution)/shard_map/srab,acb->srcb/dot_general | solution.py:28
  203.5 10.4 %convert_reduce_fusion = bf16[512,64,64]{0,1,2:T(8,128)(2,1)} fusion(f32[2,64,64]{1,0,2:T(2,128)S(1)} %copy.47, bf16[2,512,64,64]{1,2,0,3:T(8,128)(2,1)} %fusion.2, f32[2,64,64]{1,0,2:T(2,128)S(1)} %copy.46, bf16[64,64,64]{0,1,2:T(8,128)(2,1)} %get-tuple-element.16, bf16[64,64,64]{0,1,2:T(8,128)(2,1)} %get-tuple-element.17), kind=kOutput, calls=%fused_computation.19 | convolution fusion | flops 1096810496 | bytes 13697024 | tf_op jit(solution)/shard_map/srab,acb->srcb/dot_general | solution.py:28
  213.9 4.5 %copy.48 = bf16[512,64,64]{0,2,1:T(8,128)(2,1)S(1)} copy(bf16[512,64,64]{0,1,2:T(8,128)(2,1)} %convert_reduce_fusion) | data formatting | bytes 8388608 | tf_op jit(solution)/shard_map/srw,wo->ro/reduce_sum | solution.py:41
  218.4 2.0 fusion.26
  220.4 0.0 all-reduce.4.cloned.1.call-update
  220.5 90.1 %all-reduce.4.cloned.1.call-done = f32[512,128]{1,0:T(8,128)} async-done(((f32[512,128]{1,0:T(8,128)}), f32[512,128]{1,0:T(8,128)}) %all-reduce.4.cloned.1.call-update) | async-done | bytes 262160 | tf_op jit(solution)/shard_map/psum | solution.py:42
  310.5 1.3 dynamic-slice_multiply_fusion
  (20 shorter events, 0.1 us)
Async XLA Ops:
  6.5 211.9 %copy-start = (bf16[4096,128]{1,0:T(8,128)(2,1)S(1)}, bf16[4096,128]{1,0:T(8,128)(2,1)}, u32[]{:S(2)}) copy-start(bf16[4096,128]{1,0:T(8,128)(2,1)} %param.17) | copy-start | bytes 3145732
  6.5 178.4 %all-reduce.6.cloned.1.call-start = ((), (), s32[]{:S(2)}) async-start(), calls=%async_computation.1 | async-start | bytes 12582912 | tf_op jit(solution)/shard_map/psum | solution.py:10
  29.2 13.4 %copy-start.4 = (s32[6]{0:T(128)S(1)}, s32[6]{0:T(128)}, u32[]{:S(2)}) copy-start(s32[6]{0:T(128)} %param.11) | copy-start | bytes 76
  29.2 21.6 %copy-start.3 = (s32[2,6]{1,0:T(2,128)S(1)}, s32[2,6]{1,0:T(2,128)}, u32[]{:S(2)}) copy-start(s32[2,6]{1,0:T(2,128)} %param.13) | copy-start | bytes 148
  39.4 26.3 %copy-start.5 = (s32[512]{0:T(512)S(1)}, s32[512]{0:T(512)}, u32[]{:S(2)}) copy-start(s32[512]{0:T(512)} %param.10) | copy-start | bytes 6148
  42.3 268.2 %all-reduce.4.cloned.1.call-start = ((), (), s32[]{:S(2)}) async-start(), calls=%async_computation | async-start | bytes 524288 | tf_op jit(solution)/shard_map/psum | solution.py:42
  185.0 8.7 %copy-start.1 = (bf16[64,64,64]{0,1,2:T(8,128)(2,1)S(1)}, bf16[64,64,64]{0,1,2:T(8,128)(2,1)}, u32[]{:S(2)}) copy-start(bf16[64,64,64]{0,1,2:T(8,128)(2,1)} %get-tuple-element.14) | copy-start | bytes 1572868
  185.0 8.7 %copy-start.2 = (bf16[64,64,64]{0,1,2:T(8,128)(2,1)S(1)}, bf16[64,64,64]{0,1,2:T(8,128)(2,1)}, u32[]{:S(2)}) copy-start(bf16[64,64,64]{0,1,2:T(8,128)(2,1)} %get-tuple-element.15) | copy-start | bytes 1572868
Sparse Core Ops, SparseCore 0:
  42.4 142.4 all-reduce.5
  220.6 89.9 all-reduce.3
where the time goes:
time: 320 us; the launch traced here: 319 us
  waiting for transfers between devices  184 us (58%)
  local copies, waits for them, and re-layouts  67.4 us (21%)
  matrix products  30.9 us (10%)
  between operations  28.8 us (9%)
  other arithmetic  7.02 us (2%)
    psum x1, waiting for transfers between devices, spread(): return lax.psum(block, axis)  94.3 us
    psum x1, waiting for transfers between devices, local(): totals = lax.psum(partial_amps, 'slc')  90.1 us
    dot_general x3, matrix products, local(): jnp.einsum('srab,acb->srcb', states.reshape(slice_count, row_total, bond_...  28.9 us
    reshape x12, local copies, waits for them, and re-layouts, local(): branch.reshape(bond_dim, bond_dim, bond_dim)  28 us
    gather x2, local copies, waits for them, and re-layouts, local(): starts = jnp.take(boundary, bitstrings, axis=0)  17.9 us
  transfers between devices with their start and end apart: 2, of which 2 were waited for; matrix products, arithmetic and copies ran while one was open for 11% of the time, Pallas kernels for 0%

commit v1 on v0

--- a/solution.py
+++ b/solution.py
@@ -39,7 +39,9 @@
     inverse = 1.0 / math.sqrt(slice_count * group_count)
     share_rows = row_total // group_count
     partial_amps = jnp.einsum("srw,wo->ro", states, closing, preferred_element_type=jnp.float32)
-    totals = lax.psum(partial_amps, "slc")
+    totals = partial_amps
+    for hop in (1, 2, 4, 8):
+        totals = totals + lax.ppermute(totals, "slc", [(dev, dev ^ hop) for dev in range(16)])
     summed = lax.dynamic_slice_in_dim(totals, my_index * share_rows, share_rows, 0)
     return summed * inverse
 

time: 320 us -> 259 us (0.81)
  waiting for transfers between devices: 184 us -> 120 us
  starting transfers between devices: 0.22 us -> 5.63 us
    psum x1 -> x0, waiting for transfers between devices: 90.1 us -> none  [local(): totals = lax.psum(partial_amps, 'slc')]
    ppermute x0 -> x4, waiting for transfers between devices: none -> 25.2 us  [local(): lax.ppermute(totals, 'slc', [(dev, dev ^ hop) for dev in range(16)])]
    ppermute x0 -> x4, starting transfers between devices: none -> 5.63 us  [local(): lax.ppermute(totals, 'slc', [(dev, dev ^ hop) for dev in range(16)])]
  transfers between devices with their start and end apart: 2 -> 5, of which waited for: 2 -> 5; matrix products, arithmetic and copies ran while one was open for 11% -> 14% of each run, Pallas kernels for 0% -> 0%
where the time goes in v1:
time: 259 us; the launch traced here: 258 us
  waiting for transfers between devices  120 us (46%)
  local copies, waits for them, and re-layouts  67.4 us (26%)
  matrix products  30.2 us (12%)
  between operations  28.7 us (11%)
  other arithmetic  6.4 us (2%)
  starting transfers between devices  5.63 us (2%)
    psum x1, waiting for transfers between devices, spread(): return lax.psum(block, axis)  94.4 us
    dot_general x3, matrix products, local(): jnp.einsum('srab,acb->srcb', states.reshape(slice_count, row_total, bond_...  28.9 us
    reshape x12, local copies, waits for them, and re-layouts, local(): branch.reshape(bond_dim, bond_dim, bond_dim)  28 us
    ppermute x4, waiting for transfers between devices, local(): lax.ppermute(totals, 'slc', [(dev, dev ^ hop) for dev in range(16)])  25.2 us
    gather x2, local copies, waits for them, and re-layouts, local(): starts = jnp.take(boundary, bitstrings, axis=0)  17.9 us
    gather x6, local copies, waits for them, and re-layouts, local(): jnp.take(table, slice_assign[:, section_idx], axis=0).astype(jnp.float32)  5.73 us
    ppermute x4, starting transfers between devices, local(): lax.ppermute(totals, 'slc', [(dev, dev ^ hop) for dev in range(16)])  5.63 us
  transfers between devices with their start and end apart: 5, of which 5 were waited for; matrix products, arithmetic and copies ran while one was open for 14% of the time, Pallas kernels for 0%

profile of v1, /device:TPU:0, one launch (start us, length us, event | category | flops | bytes accessed | tf_op | source)
XLA Modules:
  0.0 257.9 jit_solution(15394394379374392885)
XLA Ops:
  6.5 0.0 all-reduce.3.cloned.1.call-start
  6.5 1.6 fusion.26
  11.9 2.4 broadcast_select_fusion.6
  14.3 2.1 reshape.99
  16.3 2.9 %copy.34 = bf16[64,64,64]{0,1,2:T(8,128)(2,1)} copy(bf16[64,64,64]{2,1,0:T(8,128)(2,1)S(1)} %reshape.99) | data formatting | bytes 1048576 | tf_op jit(solution)/shard_map/reshape | solution.py:31
  19.2 2.1 reshape.102
  21.3 2.9 %copy.37 = bf16[64,64,64]{0,1,2:T(8,128)(2,1)} copy(bf16[64,64,64]{2,1,0:T(8,128)(2,1)S(1)} %reshape.102) | data formatting | bytes 1048576 | tf_op jit(solution)/shard_map/reshape | solution.py:31
  24.2 2.1 reshape.101
  26.3 2.9 %copy.36 = bf16[64,64,64]{0,1,2:T(8,128)(2,1)} copy(bf16[64,64,64]{2,1,0:T(8,128)(2,1)S(1)} %reshape.101) | data formatting | bytes 1048576 | tf_op jit(solution)/shard_map/reshape | solution.py:31
  29.2 2.1 reshape.100
  31.3 2.9 %copy.35 = bf16[64,64,64]{0,1,2:T(8,128)(2,1)} copy(bf16[64,64,64]{2,1,0:T(8,128)(2,1)S(1)} %reshape.100) | data formatting | bytes 1048576 | tf_op jit(solution)/shard_map/reshape | solution.py:31
  34.2 1.1 reshape.104
  35.3 2.9 %copy.39 = bf16[64,64,64]{0,1,2:T(8,128)(2,1)} copy(bf16[64,64,64]{2,1,0:T(8,128)(2,1)S(1)} %reshape.104) | data formatting | bytes 1048576 | tf_op jit(solution)/shard_map/reshape | solution.py:31
  38.3 1.1 reshape.103
  39.4 0.0 copy-start.5
  39.4 2.9 %copy.38 = bf16[64,64,64]{0,1,2:T(8,128)(2,1)} copy(bf16[64,64,64]{2,1,0:T(8,128)(2,1)S(1)} %reshape.103) | data formatting | bytes 1048576 | tf_op jit(solution)/shard_map/reshape | solution.py:31
  42.3 0.0 all-reduce.3.cloned.1.call-update
  42.4 0.7 fusion.25
  50.6 0.0 copy-done.3
  50.6 0.3 slice_reduce_fusion.1
  54.8 3.1 %dynamic-slice_bitcast_fusion.1 = (bf16[64,4096]{1,0:T(8,128)(2,1)}, bf16[64,4096]{1,0:T(8,128)(2,1)}, bf16[64,4096]{1,0:T(8,128)(2,1)S(1)}, bf16[64,4096]{1,0:T...) fusion(bf16[6,64,4096]{2,1,0:T(8,128)(2,1)} %param.16, s32[]{:T(128)S(6)} %select_n.122, ...), kind=kLoop, calls=%fused_computation.29 | loop fusion | bytes 6291480 | tf_op jit(solution)/shard_map/jit(dynamic_index_in_dim)/squeeze | solution.py:34
  57.9 1.7 gather_fusion.5
  59.6 0.1 fusion.22
  59.7 0.1 reshape.115
  59.8 0.1 copy.46
  59.9 1.7 gather_fusion.4
  61.6 0.1 fusion.21
  61.7 0.1 reshape.114
  61.8 0.1 copy.45
  61.9 0.6 gather_fusion.3
  62.5 0.1 fusion.20
  62.5 0.1 reshape.113
  62.7 0.1 copy.44
  62.7 0.6 gather_fusion.2
  63.3 0.1 fusion.19
  63.4 0.1 reshape.112
  63.5 0.1 copy.43
  63.6 0.6 gather_fusion.1
  64.2 0.1 fusion.18
  64.3 0.1 reshape.111
  64.4 0.1 copy.42
  64.5 0.6 gather_fusion.6
  65.1 0.1 fusion.23
  65.2 0.1 reshape.116
  65.3 0.1 copy.47
  65.4 11.4 %gather_fusion = bf16[512,4096]{1,0:T(8,128)(2,1)} fusion(bf16[512,4096]{1,0:T(8,128)(2,1)} %param.14, s32[1024]{0:T(1024)S(1)} %pad_clamp_fusion.6), kind=kCustom, calls=%fused_computation.6 | custom fusion | bytes 8390656 | tf_op jit(solution)/shard_map/jit(_take)/gather | solution.py:23
  76.8 6.6 %copy.40 = bf16[512,4096]{0,1:T(8,128)(2,1)} copy(bf16[512,4096]{1,0:T(8,128)(2,1)} %gather_fusion) | data formatting | bytes 8388608 | tf_op jit(solution)/shard_map/jit(_take)/gather | solution.py:23
  83.3 2.7 %broadcast_select_fusion = bf16[512,64,64]{0,2,1:T(8,128)(2,1)S(1)} fusion(bf16[512,64,64]{0,2,1:T(8,128)(2,1)} %bitcast.97, pred[512]{0:T(512)(128)(4,1)S(1)} %compare_and_fusion.6), kind=kLoop, calls=%fused_computation.21 | loop fusion | flops 2097152 | bytes 8389120 | tf_op jit(solution)/shard_map/jit(_take)/select_n | solution.py:23
  86.0 4.4 %copy.41 = bf16[512,64,64]{0,1,2:T(8,128)(2,1)} copy(bf16[512,64,64]{0,2,1:T(8,128)(2,1)S(1)} %broadcast_select_fusion) | data formatting | bytes 8388608 | tf_op jit(solution)/shard_map/jit(_take)/select_n | solution.py:23
  90.4 94.4 %all-reduce.3.cloned.1.call-done = (bf16[64,64,64]{0,1,2:T(8,128)(2,1)}, bf16[64,64,64]{0,1,2:T(8,128)(2,1)}, bf16[64,64,64]{0,1,2:T(8,128)(2,1)}, bf16[64,64,64...) async-done(((bf16[64,64,64]{0,1,2:T(8,128)(2,1)}, bf16[64,64,64]{0,1,2:T(8,128)(2,1)}, bf16[64,64,64]{0,1,2:T(8,128)(2,1)}, ...) | async-done | bytes 3145744 | tf_op jit(solution)/shard_map/psum | solution.py:10
  184.8 8.7 %fusion.4 = bf16[2,512,64,64]{1,2,0,3:T(8,128)(2,1)} fusion(f32[2,64,64]{1,0,2:T(2,128)S(1)} %copy.43, f32[2,64,64]{1,0,2:T(2,128)S(1)} %copy.42, bf16[512,64,64]{0,1,2:T(8,128)(2,1)} %copy.41, bf16[64,64,64]{0,1,2:T(8,128)(2,1)} %get-tuple-element.12, bf16[64,64,64]{0,1,2:T(8,128)(2,1)} %get-tuple-element.13), kind=kOutput, calls=%fused_computation.16 | convolution fusion | flops 1090519040 | bytes 13697024 | tf_op jit(solution)/shard_map/srab,acb->srcb/dot_general | solution.py:28
  193.5 10.0 %fusion.2 = bf16[2,512,64,64]{1,2,0,3:T(8,128)(2,1)} fusion(f32[2,64,64]{1,0,2:T(2,128)S(1)} %copy.45, bf16[2,512,64,64]{1,2,0,3:T(8,128)(2,1)} %fusion.4, f32[2,64,64]{1,0,2:T(2,128)S(1)} %copy.44, bf16[64,64,64]{0,1,2:T(8,128)(2,1)S(1)} %copy-done.1, bf16[64,64,64]{0,1,2:T(8,128)(2,1)S(1)} %copy-done.2), kind=kOutput, calls=%fused_computation.12 | convolution fusion | flops 1090519040 | bytes 17891328 | tf_op jit(solution)/shard_map/srab,acb->srcb/dot_general | solution.py:28
  203.5 10.2 %convert_reduce_fusion = bf16[512,64,64]{0,1,2:T(8,128)(2,1)} fusion(f32[2,64,64]{1,0,2:T(2,128)S(1)} %copy.47, bf16[2,512,64,64]{1,2,0,3:T(8,128)(2,1)} %fusion.2, f32[2,64,64]{1,0,2:T(2,128)S(1)} %copy.46, bf16[64,64,64]{0,1,2:T(8,128)(2,1)} %get-tuple-element.16, bf16[64,64,64]{0,1,2:T(8,128)(2,1)} %get-tuple-element.17), kind=kOutput, calls=%fused_computation.19 | convolution fusion | flops 1096810496 | bytes 13697024 | tf_op jit(solution)/shard_map/srab,acb->srcb/dot_general | solution.py:28
  213.7 4.5 %copy.48 = bf16[512,64,64]{0,2,1:T(8,128)(2,1)S(1)} copy(bf16[512,64,64]{0,1,2:T(8,128)(2,1)} %convert_reduce_fusion) | data formatting | bytes 8388608 | tf_op jit(solution)/shard_map/srw,wo->ro/reduce_sum | solution.py:41
  218.3 1.3 fusion.27
  219.6 0.1 collective-permute-start
  219.6 1.5 collective-permute-done
  221.2 1.5 collective-permute-start.1
  222.7 6.9 %collective-permute-done.1 = f32[512,128]{1,0:T(8,128)S(1)} collective-permute-done((f32[512,128]{1,0:T(8,128)S(1)}, f32[512,128]{1,0:T(8,128)S(1)}, u32[]{:S(2)}, u32[]{:S(2)}) %collective-permute-start.1) | collective-permute-done | bytes 262176 | tf_op jit(solution)/shard_map/ppermute | solution.py:44
  229.6 1.6 collective-permute-start.2
  231.2 6.0 %collective-permute-done.2 = f32[512,128]{1,0:T(8,128)S(1)} collective-permute-done((f32[512,128]{1,0:T(8,128)S(1)}, f32[512,128]{1,0:T(8,128)S(1)}, u32[]{:S(2)}, u32[]{:S(2)}) %collective-permute-start.2) | collective-permute-done | bytes 262176 | tf_op jit(solution)/shard_map/ppermute | solution.py:44
  237.2 2.5 collective-permute-start.3
  239.7 10.8 %collective-permute-done.3 = f32[512,128]{1,0:T(8,128)S(1)} collective-permute-done((f32[512,128]{1,0:T(8,128)S(1)}, f32[512,128]{1,0:T(8,128)S(1)}, u32[]{:S(2)}, u32[]{:S(2)}) %collective-permute-start.3) | collective-permute-done | bytes 262176 | tf_op jit(solution)/shard_map/ppermute | solution.py:44
  250.4 0.6 fusion.24
  (28 shorter events, 0.2 us)
Async XLA Ops:
  6.5 211.7 %copy-start = (bf16[4096,128]{1,0:T(8,128)(2,1)S(1)}, bf16[4096,128]{1,0:T(8,128)(2,1)}, u32[]{:S(2)}) copy-start(bf16[4096,128]{1,0:T(8,128)(2,1)} %param.17) | copy-start | bytes 3145732
  6.5 178.3 %all-reduce.3.cloned.1.call-start = ((), (), s32[]{:S(2)}) async-start(), calls=%async_computation | async-start | bytes 12582912 | tf_op jit(solution)/shard_map/psum | solution.py:10
  29.2 13.2 %copy-start.4 = (s32[6]{0:T(128)S(1)}, s32[6]{0:T(128)}, u32[]{:S(2)}) copy-start(s32[6]{0:T(128)} %param.11) | copy-start | bytes 76
  29.2 21.4 %copy-start.3 = (s32[2,6]{1,0:T(2,128)S(1)}, s32[2,6]{1,0:T(2,128)}, u32[]{:S(2)}) copy-start(s32[2,6]{1,0:T(2,128)} %param.13) | copy-start | bytes 148
  39.4 26.0 %copy-start.5 = (s32[512]{0:T(512)S(1)}, s32[512]{0:T(512)}, u32[]{:S(2)}) copy-start(s32[512]{0:T(512)} %param.10) | copy-start | bytes 6148
  184.8 8.7 %copy-start.1 = (bf16[64,64,64]{0,1,2:T(8,128)(2,1)S(1)}, bf16[64,64,64]{0,1,2:T(8,128)(2,1)}, u32[]{:S(2)}) copy-start(bf16[64,64,64]{0,1,2:T(8,128)(2,1)} %get-tuple-element.14) | copy-start | bytes 1572868
  184.8 8.7 %copy-start.2 = (bf16[64,64,64]{0,1,2:T(8,128)(2,1)S(1)}, bf16[64,64,64]{0,1,2:T(8,128)(2,1)}, u32[]{:S(2)}) copy-start(bf16[64,64,64]{0,1,2:T(8,128)(2,1)} %get-tuple-element.15) | copy-start | bytes 1572868
  219.6 1.6 collective-permute-start
  221.2 8.4 %collective-permute-start.1 = (f32[512,128]{1,0:T(8,128)S(1)}, f32[512,128]{1,0:T(8,128)S(1)}, u32[]{:S(2)}, u32[]{:S(2)}) collective-permute-start(f32[512,128]{1,0:T(8,128)S(1)} %add.65), channel_id=1, source_target_pairs={{0,2},{1,3},{2,0},{3,1},{4,6},{5,7},{6,4},{7,5},{8,10},{9,11},{10,... | collective-permute-start | bytes 786440 | tf_op jit(solution)/shard_map/ppermute | solution.py:44
  229.6 7.6 %collective-permute-start.2 = (f32[512,128]{1,0:T(8,128)S(1)}, f32[512,128]{1,0:T(8,128)S(1)}, u32[]{:S(2)}, u32[]{:S(2)}) collective-permute-start(f32[512,128]{1,0:T(8,128)S(1)} %add.66), channel_id=1, source_target_pairs={{0,4},{1,5},{2,6},{3,7},{4,0},{5,1},{6,2},{7,3},{8,12},{9,13},{10,... | collective-permute-start | bytes 786440 | tf_op jit(solution)/shard_map/ppermute | solution.py:44
  237.2 13.2 %collective-permute-start.3 = (f32[512,128]{1,0:T(8,128)S(1)}, f32[512,128]{1,0:T(8,128)S(1)}, u32[]{:S(2)}, u32[]{:S(2)}) collective-permute-start(f32[512,128]{1,0:T(8,128)S(1)} %add.67), channel_id=1, source_target_pairs={{0,8},{1,9},{2,10},{3,11},{4,12},{5,13},{6,14},{7,15},{8,0},{9,1},... | collective-permute-start | bytes 786440 | tf_op jit(solution)/shard_map/ppermute | solution.py:44
Sparse Core Ops, SparseCore 0:
  42.5 142.2 all-reduce.2
